TPU v7x, 32 devices: a whole 2x2x4 slice. The times are simulated.
32 devices in a mesh: dp: 8 (over y, x, core), mp: 4 (over z).
Axes of the slice: x: 2, y: 2, z: 4, core: 2. Of those that a mesh axis runs over, the one named last changes fastest.
Arguments:
- pooled: bfloat16 [2048, 3584], P('dp', 'mp'), may hold values from -4 to 4
- w_out: bfloat16 [3584, 3584], P('mp'), may hold values from -0.028931878 to 0.028931878
- assignments: int32 [2048], P('dp'), may hold values from 0 to 4095
- ema_sums: float32 [4096, 3584], P('mp', 'dp'), may hold values from -0.40089186 to 0.40089186
- ema_counts: float32 [4096], P('mp'), may hold values from 1 to 8
Outputs:
- distances: float32 [2048, 4096], P('dp', 'mp')
- new_sums: float32 [4096, 3584], P('mp', 'dp')
- new_counts: float32 [4096], P('mp')
- new_centroids: bfloat16 [4096, 3584], P('mp', 'dp')
All inputs are finite; a program needn't handle non-finite values.
Results may differ from a plain program's by a relative error of at most 0.0011.
Values may be sent and summed in bfloat16 or wider, within the bound.
A program may use at most 64 MiB of HBM per device.

v0:
```python
import math
import jax
import jax.numpy as jnp
from jax import lax
from jax.sharding import PartitionSpec as P

EPSILON = 1e-06
EMA_DECAY = 0.9


def body(pooled, w_out, assignments, ema_sums, ema_counts):
    partial_value = jnp.dot(pooled, w_out, preferred_element_type=jnp.float32)
    projected = lax.psum(partial_value, "mp")
    inverse_norm = 1.0 / jnp.sqrt(jnp.sum(projected * projected, axis=1, keepdims=True) + EPSILON)
    embedded = (projected * inverse_norm).astype(jnp.bfloat16)
    local_centers = ema_sums.shape[0]
    doc_rows = embedded.shape[0]
    centers = (ema_sums / ema_counts[:, None]).astype(jnp.bfloat16)
    column_piece = lax.all_gather(centers, "dp", axis=1, tiled=True)
    products = lax.dot_general(
        embedded, column_piece, (((1,), (1,)), ((), ())), preferred_element_type=jnp.float32
    )
    piece_wide = column_piece.astype(jnp.float32)
    center_norms = jnp.sum(piece_wide * piece_wide, axis=1)
    products, center_norms = (products, center_norms)
    embed_wide = embedded.astype(jnp.float32)
    doc_norms = jnp.sum(embed_wide * embed_wide, axis=1)
    distances = doc_norms[:, None] + center_norms[None, :] - 2.0 * products
    first_center = lax.axis_index("mp") * local_centers
    center_ids = first_center + jnp.arange(local_centers, dtype=jnp.int32)
    feature_cols = ema_sums.shape[1]
    every_assign = lax.all_gather(assignments, "dp", axis=0, tiled=True)
    own_columns = lax.all_to_all(embedded, "dp", split_axis=1, concat_axis=0, tiled=True)
    shard_count = lax.axis_size("dp")
    group_size = math.gcd(shard_count, max(1, 2048 // doc_rows))
    block_rows = group_size * doc_rows
    turns = shard_count // group_size

    def add_block(block_index, totals):
        sums_now, counts_now = totals
        block_assign = lax.dynamic_slice_in_dim(
            every_assign, block_index * block_rows, block_rows, 0
        )
        block_columns = lax.dynamic_slice_in_dim(
            own_columns, block_index * block_rows, block_rows, 0
        )
        one_hot = (block_assign[None, :] == center_ids[:, None]).astype(jnp.bfloat16)
        sums_now = sums_now + jnp.dot(one_hot, block_columns, preferred_element_type=jnp.float32)
        counts_now = counts_now + jnp.sum(one_hot, axis=1, dtype=jnp.float32)
        return (sums_now, counts_now)

    start_sums = (
        jnp.zeros((local_centers, feature_cols), jnp.float32),
        jnp.zeros((local_centers,), jnp.float32),
    )
    batch_sums, batch_counts = lax.fori_loop(0, turns, add_block, start_sums)
    new_counts = EMA_DECAY * ema_counts + (1.0 - EMA_DECAY) * batch_counts
    new_sums = EMA_DECAY * ema_sums + (1.0 - EMA_DECAY) * batch_sums
    new_centroids = (new_sums / new_counts[:, None]).astype(jnp.bfloat16)
    return (distances, new_sums, new_counts, new_centroids)


def solution(mesh):
    return jax.shard_map(
        body,
        mesh=mesh,
        in_specs=(P("dp", "mp"), P("mp", None), P("dp"), P("mp", "dp"), P("mp")),
        out_specs=(P("dp", "mp"), P("mp", "dp"), P("mp"), P("mp", "dp")),
        check_vma=False,
    )
```

profile of v0, /device:TPU:0, one launch (start us, length us, event | category | flops | bytes accessed | tf_op | source)
XLA Modules:
  0.0 215.6 jit_solution(4043559094026590558)
XLA Ops:
  8.0 0.0 copy-start
  8.0 0.0 all-reduce.2.cloned.1.call-start
  8.1 1.0 copy-done
  9.0 6.8 %fusion.7 = f32[256,3584]{1,0:T(8,128)} fusion(bf16[256,896]{1,0:T(8,128)(2,1)S(1)} %copy-done, bf16[896,3584]{1,0:T(8,128)(2,1)} %param.6), kind=kOutput, calls=%fused_computation.18 | convolution fusion | flops 1644167168 | bytes 10551296 | tf_op jit(solution)/shard_map/dot_general | solution.py:12
  15.8 0.0 copy-start.5
  15.8 0.0 all-reduce.2.cloned.1.call-update
  15.8 0.0 all-gather.3.cloned.1.call-start
  15.9 1.4 copy-done.5
  17.3 0.0 copy-done.7
  17.3 1.1 divide_convert_fusion.1
  18.5 0.0 all-gather.3.cloned.1.call-update
  18.5 138.3 %all-reduce.2.cloned.1.call-done = f32[256,3584]{1,0:T(8,128)} async-done(((f32[256,3584]{1,0:T(8,128)}), f32[256,3584]{1,0:T(8,128)}) %all-reduce.2.cloned.1.call-update) | async-done | bytes 3670032 | tf_op jit(solution)/shard_map/psum | solution.py:13
  156.7 2.5 %multiply_reduce_fusion.2 = f32[256]{0:T(256)S(1)} fusion(f32[256,3584]{1,0:T(8,128)} %all-reduce.2.cloned.1.call-done), kind=kLoop, calls=%fused_computation.9 | loop fusion | flops 1834752 | bytes 3671040 | tf_op jit(solution)/shard_map/reduce_sum | solution.py:14
  159.3 0.6 copy-done.1
  159.9 0.6 multiply_reduce_fusion.1
  160.5 2.5 %copy.13 = bf16[256,3584]{0,1:T(8,128)(2,1)} copy(bf16[256,3584]{1,0:T(8,128)(2,1)S(1)} %get-tuple-element.19) | data formatting | bytes 3670016 | tf_op jit(solution)/shard_map/convert_element_type | solution.py:15
  162.9 0.0 copy-done.3
  162.9 3.8 %all-to-all-start = ((bf16[256,8,448]{0,2,1:T(8,128)(2,1)}), bf16[256,8,448]{0,2,1:T(8,128)(2,1)S(1)}, u32[]{:S(2)}, u32[]{:S(2)}) async-start(bf16[256,8,448]{0,2,1:T(8,128)(2,1)} %bitcast.12), calls=%async_computation | async-start | bytes 3670016 | tf_op jit(solution)/shard_map/all_to_all | solution.py:33
  166.7 0.0 copy-done.9
  166.7 26.9 %all-gather = s32[8,1,256]{2,1,0:T(1,128)S(1)} all-gather(s32[1,1,256]{2,1,0:T(1,128)S(1)} %bitcast.16), channel_id=1, replica_groups=mesh['dp'=8,'mp'=4] {'dp'}, dimensions={0}, use_global_device_ids=true | all-gather | bytes 9216 | tf_op jit(solution)/shard_map/all_gather | solution.py:32
  193.6 1.0 convert_reduce_fusion
  194.6 0.0 copy-start.8
  194.6 0.0 all-to-all-done
  194.6 0.0 copy-start.6
  194.6 0.2 copy.15
  194.8 1.3 copy-done.6
  196.1 3.8 %divide_convert_fusion = (bf16[1024,448]{0,1:T(8,128)(2,1)}, f32[1024,448]{0,1:T(8,128)}) fusion(f32[1024]{0:T(1024)S(1)} %multiply_add_fusion.1, bf16[2048,448]{0,1:T(8,128)(2,1)S(1)} %bitcast.13, s32[2048]{0:T(1024)S(1)} %bitcast.15, s32[1024]{0:T(1024)S(1)} %iota_add_fusion, f32[1024,448]{0,1:T(8,128)S(1)} %copy-done.6), kind=kOutput, calls=%fused_computation.10 | convolution fusion | flops 1883439104 | bytes 6438912 | tf_op jit(solution)/shard_map/while/body/eval_jaxpr/dot_general | solution.py:48
  199.9 0.0 copy-done.8
  199.9 4.7 %multiply_reduce_fusion = f32[1024]{0:T(1024)S(1)} fusion(bf16[1024,3584]{0,1:T(8,128)(2,1)} %all-gather.3.cloned.1.call-done), kind=kLoop, calls=%fused_computation | loop fusion | flops 11009024 | bytes 7344128 | tf_op jit(solution)/shard_map/reduce_sum | solution.py:24
  204.6 0.0 copy-done.4
  204.6 0.4 copy-done.2
  205.1 3.0 %fusion.6 = f32[256,1024]{1,0:T(8,128)} fusion(bf16[256,3584]{1,0:T(8,128)(2,1)S(1)} %copy-done.4, bf16[1024,3584]{0,1:T(8,128)(2,1)S(1)} %copy-done.2, f32[1024]{0:T(1024)S(1)} %multiply_reduce_fusion, f32[256]{0:T(256)S(1)} %get-tuple-element.18), kind=kOutput, calls=%fused_computation.14 | convolution fusion | flops 1879834624 | bytes 10228736 | tf_op jit(solution)/shard_map/dot_general | solution.py:20
  (10 shorter events, 0.0 us)
Async XLA Ops:
  8.0 1.0 copy-start
  8.0 148.7 %all-reduce.2.cloned.1.call-start = ((), (), s32[]{:S(2)}) async-start(), calls=%async_computation.1 | async-start | bytes 7340032 | tf_op jit(solution)/shard_map/psum | solution.py:13
  15.8 1.5 copy-start.5
  15.8 1.5 copy-start.7
  15.8 184.1 %all-gather.3.cloned.1.call-start = ((), (), s32[]{:S(2)}) async-start(), calls=%async_computation.2 | async-start | bytes 8257536 | tf_op jit(solution)/shard_map/all_gather | solution.py:19
  156.7 3.1 %copy-start.1 = (f32[256,3584]{1,0:T(8,128)S(1)}, f32[256,3584]{1,0:T(8,128)}, u32[]{:S(2)}) copy-start(f32[256,3584]{1,0:T(8,128)} %all-reduce.2.cloned.1.call-done) | copy-start | bytes 11010052
  160.5 2.5 %copy-start.3 = (bf16[256,3584]{1,0:T(8,128)(2,1)}, bf16[256,3584]{1,0:T(8,128)(2,1)S(1)}, u32[]{:S(2)}) copy-start(bf16[256,3584]{1,0:T(8,128)(2,1)S(1)} %get-tuple-element.19) | copy-start | bytes 5505028
  162.9 3.8 %copy-start.9 = (s32[256]{0:T(256)S(1)}, s32[256]{0:T(256)}, u32[]{:S(2)}) copy-start(s32[256]{0:T(256)} %param.7) | copy-start | bytes 3076
  162.9 31.6 %all-to-all-start = ((bf16[256,8,448]{0,2,1:T(8,128)(2,1)}), bf16[256,8,448]{0,2,1:T(8,128)(2,1)S(1)}, u32[]{:S(2)}, u32[]{:S(2)}) async-start(bf16[256,8,448]{0,2,1:T(8,128)(2,1)} %bitcast.12), calls=%async_computation | async-start | bytes 3670016 | tf_op jit(solution)/shard_map/all_to_all | solution.py:33
  194.6 5.3 %copy-start.8 = (f32[1024]{0:T(1024)}, f32[1024]{0:T(1024)S(1)}, u32[]{:S(2)}) copy-start(f32[1024]{0:T(1024)S(1)} %multiply_add_fusion.1) | copy-start | bytes 12292
  194.6 1.5 copy-start.6
  196.1 8.5 %copy-start.4 = (bf16[256,3584]{1,0:T(8,128)(2,1)S(1)}, bf16[256,3584]{1,0:T(8,128)(2,1)}, u32[]{:S(2)}) copy-start(bf16[256,3584]{1,0:T(8,128)(2,1)} %copy-done.3) | copy-start | bytes 5505028
  199.9 5.2 %copy-start.2 = (bf16[1024,3584]{0,1:T(8,128)(2,1)S(1)}, bf16[1024,3584]{0,1:T(8,128)(2,1)}, u32[]{:S(2)}) copy-start(bf16[1024,3584]{0,1:T(8,128)(2,1)} %all-gather.3.cloned.1.call-done) | copy-start | bytes 22020100
Sparse Core Ops, SparseCore 0:
  16.0 140.7 all-reduce.1
Sparse Core Ops, SparseCore 1:
  18.8 52.4 all-gather.2
where the time goes:
time: 216 us
  waiting for transfers between devices  138 us (64%)
  blocking collectives  26.9 us (12%)
  between operations  15.5 us (7%)
  matrix products  13.6 us (6%)
  other arithmetic  9.94 us (5%)
  local copies, waits for them, and re-layouts  7.42 us (3%)
  starting transfers between devices  3.87 us (2%)
    psum x1, waiting for transfers between devices, body(): projected = lax.psum(partial_value, 'mp')  138 us
    all_gather x1, blocking collectives, body(): every_assign = lax.all_gather(assignments, 'dp', axis=0, tiled=True)  26.9 us
    dot_general x1, matrix products, body(): partial_value = jnp.dot(pooled, w_out, preferred_element_type=jnp.float32)  6.79 us
    reduce_sum x1, other arithmetic, body(): center_norms = jnp.sum(piece_wide * piece_wide, axis=1)  4.74 us
    unnamed x20, local copies, waits for them, and re-layouts  4.72 us
  transfers between devices with their start and end apart: 3, of which 1 were waited for; matrix products, arithmetic and copies ran while one was open for 5% of the time, Pallas kernels for 0%

commit v1 on v0

--- a/solution.py
+++ b/solution.py
@@ -3,6 +3,7 @@
 import jax.numpy as jnp
 from jax import lax
 from jax.sharding import PartitionSpec as P
+from jax.lax import all_gather
 
 EPSILON = 1e-06
 EMA_DECAY = 0.9
@@ -10,7 +11,7 @@
 
 def body(pooled, w_out, assignments, ema_sums, ema_counts):
     partial_value = jnp.dot(pooled, w_out, preferred_element_type=jnp.float32)
-    projected = lax.psum(partial_value, "mp")
+    projected = all_gather(partial_value, "mp").sum(axis=0)
     inverse_norm = 1.0 / jnp.sqrt(jnp.sum(projected * projected, axis=1, keepdims=True) + EPSILON)
     embedded = (projected * inverse_norm).astype(jnp.bfloat16)
     local_centers = ema_sums.shape[0]

time: 216 us -> 359 us (1.66)
  waiting for transfers between devices: 138 us -> 286 us
  blocking collectives: 26.9 us -> 10.4 us
  other arithmetic: 9.94 us -> 20.4 us
    all_gather x0 -> x1, waiting for transfers between devices: none -> 241 us  [body(): projected = all_gather(partial_value, 'mp').sum(axis=0)]
    psum x1 -> x0, waiting for transfers between devices: 138 us -> none  [body(): projected = lax.psum(partial_value, 'mp')]
    all_gather x1, waiting for transfers between devices: 0.01 us -> 44.4 us  [body(): column_piece = lax.all_gather(centers, 'dp', axis=1, tiled=True)]
    all_gather x1, blocking collectives: 26.9 us -> 10.4 us  [body(): every_assign = lax.all_gather(assignments, 'dp', axis=0, tiled=True)]
    reduce_sum x0 -> x1, other arithmetic: none -> 8.88 us  [body(): projected = all_gather(partial_value, 'mp').sum(axis=0)]
    reduce_sum x0 -> x1, local copies, waits for them, and re-layouts: none -> 5.33 us  [body(): projected = all_gather(partial_value, 'mp').sum(axis=0)]
  transfers between devices with their start and end apart: 3 -> 3, of which waited for: 1 -> 2; matrix products, arithmetic and copies ran while one was open for 5% -> 8% of each run, Pallas kernels for 0% -> 0%
where the time goes in v1:
time: 359 us
  waiting for transfers between devices  286 us (80%)
  other arithmetic  20.4 us (6%)
  between operations  14.1 us (4%)
  matrix products  13.6 us (4%)
  local copies, waits for them, and re-layouts  10.9 us (3%)
  blocking collectives  10.4 us (3%)
  starting transfers between devices  3.67 us (1%)
    all_gather x1, waiting for transfers between devices, body(): projected = all_gather(partial_value, 'mp').sum(axis=0)  241 us
    all_gather x1, waiting for transfers between devices, body(): column_piece = lax.all_gather(centers, 'dp', axis=1, tiled=True)  44.4 us
    all_gather x1, blocking collectives, body(): every_assign = lax.all_gather(assignments, 'dp', axis=0, tiled=True)  10.4 us
    reduce_sum x1, other arithmetic, body(): projected = all_gather(partial_value, 'mp').sum(axis=0)  8.88 us
  transfers between devices with their start and end apart: 3, of which 2 were waited for; matrix products, arithmetic and copies ran while one was open for 8% of the time, Pallas kernels for 0%

profile of v1, /device:TPU:0, one launch (start us, length us, event | category | flops | bytes accessed | tf_op | source)
XLA Modules:
  0.0 358.8 jit_solution(9337845953034196079)
XLA Ops:
  7.2 0.0 copy-start
  7.2 0.0 all-gather.7.cloned.1.call-start
  7.2 1.0 copy-done
  8.2 6.7 %fusion.7 = f32[256,3584]{1,0:T(8,128)} fusion(bf16[256,896]{1,0:T(8,128)(2,1)S(1)} %copy-done, bf16[896,3584]{1,0:T(8,128)(2,1)} %param.6), kind=kOutput, calls=%fused_computation.19 | convolution fusion | flops 1644167168 | bytes 10551296 | tf_op jit(solution)/shard_map/dot_general | solution.py:13
  14.9 0.0 all-gather.7.cloned.1.call-update
  15.0 0.0 all-gather.5.cloned.1.call-start
  15.0 1.4 copy-done.4
  16.4 0.0 copy-done.6
  16.4 1.1 divide_convert_fusion.1
  17.6 0.0 all-gather.5.cloned.1.call-update
  17.6 0.0 copy-done.8
  17.6 10.4 %all-gather.1 = s32[8,1,256]{2,1,0:T(1,128)S(1)} all-gather(s32[1,1,256]{2,1,0:T(1,128)S(1)} %bitcast.17), channel_id=1, replica_groups=mesh['dp'=8,'mp'=4] {'dp'}, dimensions={0}, use_global_device_ids=true | all-gather | bytes 9216 | tf_op jit(solution)/shard_map/all_gather | solution.py:33
  28.0 1.0 convert_reduce_fusion
  29.0 0.0 copy-start.7
  29.0 241.3 %all-gather.7.cloned.1.call-done = f32[1024,3584]{1,0:T(8,128)} async-done(((f32[256,3584]{1,0:T(8,128)}), f32[1024,3584]{1,0:T(8,128)}) %all-gather.7.cloned.1.call-update) | async-done | bytes 14680080 | tf_op jit(solution)/shard_map/all_gather | solution.py:14
  270.3 8.9 %reduce_sum.48 = f32[256,3584]{1,0:T(8,128)} reduce(f32[4,256,3584]{2,1,0:T(8,128)} %bitcast.12, f32[]{:T(128)} %constant.7.clone.1), dimensions={0}, to_apply=%region_0.0 | reduce | flops 2752512 | bytes 18350084 | tf_op jit(solution)/shard_map/reduce_sum | solution.py:14
  279.2 5.3 %copy.12 = f32[256,3584]{0,1:T(8,128)} copy(f32[256,3584]{1,0:T(8,128)} %reduce_sum.48) | data formatting | bytes 7340032 | tf_op jit(solution)/shard_map/reduce_sum | solution.py:14
  284.5 2.5 multiply_reduce_fusion.2
  287.0 0.6 copy-done.2
  287.7 1.6 multiply_convert_fusion
  289.3 3.6 %all-to-all-start = ((bf16[256,8,448]{0,2,1:T(8,128)(2,1)}), bf16[256,8,448]{0,2,1:T(8,128)(2,1)S(1)}, u32[]{:S(2)}, u32[]{:S(2)}) async-start(bf16[256,8,448]{0,2,1:T(8,128)(2,1)} %multiply_convert_fusion), calls=%async_computation | async-start | bytes 3670016 | tf_op jit(solution)/shard_map/all_to_all | solution.py:34
  292.9 44.4 %all-gather.5.cloned.1.call-done = bf16[1024,3584]{0,1:T(8,128)(2,1)} async-done(((bf16[1024,448]{0,1:T(8,128)(2,1)}), bf16[1024,3584]{0,1:T(8,128)(2,1)}) %all-gather.5.cloned.1.call-update) | async-done | bytes 7340048 | tf_op jit(solution)/shard_map/all_gather | solution.py:20
  337.3 4.7 %multiply_reduce_fusion = f32[1024]{0:T(1024)S(1)} fusion(bf16[1024,3584]{0,1:T(8,128)(2,1)} %all-gather.5.cloned.1.call-done), kind=kLoop, calls=%fused_computation | loop fusion | flops 11009024 | bytes 7344128 | tf_op jit(solution)/shard_map/reduce_sum | solution.py:25
  342.0 0.0 copy-done.1
  342.0 0.5 multiply_reduce_fusion.1
  342.5 1.0 copy-done.3
  343.5 3.1 fusion.6
  346.6 0.0 all-to-all-done
  346.6 0.2 copy.14
  346.9 0.0 copy-done.7
  346.9 1.3 copy-done.5
  348.1 3.8 %divide_convert_fusion = (bf16[1024,448]{0,1:T(8,128)(2,1)}, f32[1024,448]{0,1:T(8,128)}) fusion(f32[1024]{0:T(1024)S(1)} %multiply_add_fusion.1, bf16[2048,448]{0,1:T(8,128)(2,1)S(1)} %bitcast.14, s32[2048]{0:T(1024)S(1)} %bitcast.16, s32[1024]{0:T(1024)S(1)} %iota_add_fusion, f32[1024,448]{0,1:T(8,128)S(1)} %copy-done.5), kind=kOutput, calls=%fused_computation.11 | convolution fusion | flops 1883439104 | bytes 6438912 | tf_op jit(solution)/shard_map/while/body/eval_jaxpr/dot_general | solution.py:49
  (10 shorter events, 0.0 us)
Async XLA Ops:
  7.2 1.0 copy-start
  7.2 263.1 %all-gather.7.cloned.1.call-start = ((), (), s32[]{:S(2)}) async-start(), calls=%async_computation.2 | async-start | bytes 18350080 | tf_op jit(solution)/shard_map/all_gather | solution.py:14
  14.9 1.5 copy-start.4
  14.9 1.5 copy-start.6
  14.9 2.7 copy-start.8
  15.0 322.3 %all-gather.5.cloned.1.call-start = ((), (), s32[]{:S(2)}) async-start(), calls=%async_computation.1 | async-start | bytes 8257536 | tf_op jit(solution)/shard_map/all_gather | solution.py:20
  29.0 317.9 %copy-start.7 = (f32[1024]{0:T(1024)}, f32[1024]{0:T(1024)S(1)}, u32[]{:S(2)}) copy-start(f32[1024]{0:T(1024)S(1)} %multiply_add_fusion.1) | copy-start | bytes 12292
  284.5 3.1 copy-start.2
  289.3 57.4 %all-to-all-start = ((bf16[256,8,448]{0,2,1:T(8,128)(2,1)}), bf16[256,8,448]{0,2,1:T(8,128)(2,1)S(1)}, u32[]{:S(2)}, u32[]{:S(2)}) async-start(bf16[256,8,448]{0,2,1:T(8,128)(2,1)} %multiply_convert_fusion), calls=%async_computation | async-start | bytes 3670016 | tf_op jit(solution)/shard_map/all_to_all | solution.py:34
  337.3 4.7 %copy-start.1 = (f32[256,3584]{1,0:T(8,128)S(1)}, f32[256,3584]{1,0:T(8,128)}, u32[]{:S(2)}) copy-start(f32[256,3584]{1,0:T(8,128)} %reduce_sum.48) | copy-start | bytes 11010052
  337.3 6.3 %copy-start.3 = (bf16[1024,3584]{0,1:T(8,128)(2,1)S(1)}, bf16[1024,3584]{0,1:T(8,128)(2,1)}, u32[]{:S(2)}) copy-start(bf16[1024,3584]{0,1:T(8,128)(2,1)} %all-gather.5.cloned.1.call-done) | copy-start | bytes 22020100
  346.6 1.5 copy-start.5
Sparse Core Ops, SparseCore 0:
  15.1 255.1 all-gather.6
  272.8 64.4 all-gather.4
